TPU v7x, 256 devices: a whole 4x4x8 slice. The times are simulated.
256 devices in a mesh: section: 2 (over z_lo), tile: 128 (over y, z_hi, x, core).
Axes of the slice: x: 4, y: 4, z: 8 (z_hi: 4, z_lo: 2; z = z_hi * 2 + z_lo), core: 2. Of those that a mesh axis runs over, the one named last changes fastest.
Arguments:
- coarse: bfloat16 [12, 4096, 128], P(None, 'tile'), may hold values from -6 to 6
- lift_weight: bfloat16 [128, 12], replicated, may hold values from -1.75 to 1.75
- conv_weight: bfloat16 [3, 3, 128, 128], replicated, may hold values from -0.1875 to 0.1875
- out_weight: bfloat16 [4, 128], replicated, may hold values from -0.5 to 0.5
- denoise_in: bfloat16 [128, 8], replicated, may hold values from -2 to 2
- denoise_mid: bfloat16 [128, 128], replicated, may hold values from -0.5 to 0.5
- denoise_out: bfloat16 [4, 128], replicated, may hold values from -0.5 to 0.5
- base_noise: bfloat16 [4, 4, 4096, 128], P(None, None, 'tile'), may hold values from -5 to 5
- slot_noise: bfloat16 [4, 4, 4096, 128], P(None, None, 'tile'), may hold values from -5 to 5
- extra_dest: int32 [128, 8], P('tile'), may hold values from -1 to 127, as said below
Outputs:
- moments: float32 [2, 4, 4096, 128], P('section', None, 'tile')
Inputs may be any that keep to these rules, and one draw needn't show every extreme that they name: `extra_dest`: the non-negative entries of row t come first and are consecutive device indices t + o, t + o + 1, ... (modulo 128) with 0 <= o and all of them within t to t + 8 - 1 modulo 128; the rest are -1. Every device is named exactly 4 times over all rows; some row has 8 non-negative entries.
All inputs are finite; a program needn't handle non-finite values.
Results may differ from a plain program's by a relative error of at most 0.0024.
Values may be sent and summed in bfloat16 or wider, within the bound.
A program may use at most 64 MiB of HBM per device.

v0:
```python
import functools
import math

import jax
import jax.numpy as jnp
from jax import lax
from jax.experimental import pallas as pl
from jax.experimental.pallas import tpu as pltpu
from jax.sharding import PartitionSpec as P

MESH = pl.DeviceIdType.MESH
BF = jnp.bfloat16
F32 = jnp.float32
MEMB = 4
SLOTS = 4
NSTEP = 6
REACH = 8
SIGMA_MAX = 4.0
SIGMA_MIN = 0.25
PLAN_POWER = 7.0


def sigma_table(step_count):
    upper_root = SIGMA_MAX ** (1.0 / PLAN_POWER)
    lower_root = SIGMA_MIN ** (1.0 / PLAN_POWER)
    values = []
    for position in range(step_count):
        fraction = position / (step_count - 1)
        values.append((upper_root + fraction * (lower_root - upper_root)) ** PLAN_POWER)
    values.append(0.0)
    return values


SIGMAS = sigma_table(NSTEP)


def step_factors():
    table = []
    for position in range(NSTEP):
        now, later = SIGMAS[position], SIGMAS[position + 1]
        scale = 1.0 / math.sqrt(now * now + 1.0)
        slope = (later - now) / now
        table.append((scale, 1.0 + slope * (1.0 - scale * scale), -slope * now * scale))
    return table


FACTORS = step_factors()


def pick(position, column):
    value = jnp.float32(FACTORS[NSTEP - 1][column])
    for step in range(NSTEP - 2, -1, -1):
        value = jnp.where(position == step, jnp.float32(FACTORS[step][column]), value)
    return value


def silu_of_half(half):
    return (half + half * jnp.tanh(half)).astype(BF)


def spread(rows, columns, by_row, group):
    i = lax.broadcasted_iota(jnp.int32, (rows, columns), 0)
    j = lax.broadcasted_iota(jnp.int32, (rows, columns), 1)
    same = (i // group == j) if by_row else (j // group == i)
    return same.astype(F32).astype(BF)


def kernel(
    tiles,
    coarse_ref,
    lift_ref,
    conv_ref,
    outw_ref,
    din_ref,
    dmid_ref,
    dout_ref,
    base_ref,
    slot_ref,
    dest_ref,
    out_ref,
    cv,
    wraw,
    noise,
    halo_out,
    halo_in,
    lifted,
    wconv,
    feat,
    fout,
    ein,
    emid,
    eout,
    hid1,
    hid2,
    lat,
    cond,
    gx,
    piece,
    arrived,
    swap_out,
    swap_in,
    local_sem,
    send_sem,
    recv_sem,
):
    section = lax.axis_index("section")
    tile = lax.axis_index("tile")
    half_rows = out_ref.shape[2] // 2
    cells = out_ref.shape[3]
    channels = din_ref.shape[0]
    fields = out_ref.shape[1]
    flat = fields * half_rows
    cin = lift_ref.shape[1]
    octet = half_rows // 2
    first = pl.multiple_of(section * half_rows, half_rows)

    copies = [
        pltpu.make_async_copy(coarse_ref, cv, local_sem.at[0]),
        pltpu.make_async_copy(conv_ref, wraw, local_sem.at[1]),
        pltpu.make_async_copy(
            base_ref.at[:, :, pl.ds(first, half_rows), :], noise.at[0], local_sem.at[2]
        ),
        pltpu.make_async_copy(
            slot_ref.at[:, :, pl.ds(first, half_rows), :], noise.at[1], local_sem.at[3]
        ),
    ]
    for copy in copies:
        copy.start()

    ahead = [lax.rem(tile + o, tiles) for o in range(REACH)]
    behind = [lax.rem(tile + tiles - o, tiles) for o in range(REACH)]

    barrier = pltpu.get_barrier_semaphore()
    for o in range(1, REACH):
        for other in (ahead[o], behind[o]):
            pl.semaphore_signal(barrier, inc=1, device_id={"tile": other}, device_id_type=MESH)
    pl.semaphore_signal(
        barrier, inc=1, device_id={"section": 1 - section}, device_id_type=MESH
    )

    copies[0].wait()
    top_half = section == 0
    last_row = cv[:, 2 * half_rows - 1, :].astype(F32)
    first_row = cv[:, 0, :].astype(F32)
    halo_out[...] = jnp.zeros(halo_out.shape, BF)
    halo_out[0:cin, :] = jnp.where(top_half, last_row, first_row).astype(BF)

    pl.semaphore_wait(barrier, 2 * (REACH - 1) + 1)
    halo_target = lax.rem(jnp.where(top_half, tile + 1, tile + tiles - 1), tiles)
    halo_copy = pltpu.make_async_remote_copy(
        src_ref=halo_out,
        dst_ref=halo_in,
        send_sem=send_sem.at[0],
        recv_sem=recv_sem.at[0],
        device_id={"tile": halo_target},
        device_id_type=MESH,
    )
    halo_copy.start()

    lift_half = lift_ref[...].astype(F32) * 0.5
    lift_bf = lift_half.astype(BF)
    wide = jnp.dot(lift_bf, spread(cin, cin * octet, False, octet), preferred_element_type=F32)
    lane = lax.broadcasted_iota(jnp.int32, wide.shape, 1) % octet
    own = cv[:, pl.ds(first, half_rows), :].astype(F32)
    own = jnp.concatenate(
        [
            own[:, :octet, :].reshape(cin * octet, cells),
            own[:, octet:, :].reshape(cin * octet, cells),
        ],
        axis=1,
    ).astype(BF)
    for r in range(octet):
        weight = jnp.where(lane == r, wide, 0.0).astype(BF)
        lifted[(r + 1) * channels : (r + 2) * channels, :] = silu_of_half(
            jnp.dot(weight, own, preferred_element_type=F32)
        )
    copies[1].wait()
    for a in range(3):
        for b in range(3):
            wconv[b * channels : (b + 1) * channels, a * channels : (a + 1) * channels] = (
                (wraw[a, b].astype(F32) * 0.5).T.astype(BF)
            )
    wide_in = (
        jnp.dot(
            din_ref[...], spread(2 * fields, 2 * flat, False, half_rows), preferred_element_type=F32
        )
        * 0.5
    )
    lane_in = lax.broadcasted_iota(jnp.int32, wide_in.shape, 1) % half_rows
    wide_out = jnp.dot(
        spread(flat, fields, True, half_rows), dout_ref[...], preferred_element_type=F32
    )
    row_out = lax.broadcasted_iota(jnp.int32, wide_out.shape, 0) % half_rows
    for r in range(half_rows):
        block = slice(r * channels, (r + 1) * channels)
        ein[block, :] = jnp.where(lane_in == r, wide_in, 0.0).astype(BF)
        eout[:, block] = jnp.where(row_out == r, wide_out, 0.0).astype(BF)
    mid = (dmid_ref[...].astype(F32) * 0.5).astype(BF)
    emid[...] = jnp.zeros(emid.shape, BF)
    emid[:channels, :channels] = mid
    emid[channels:, channels:] = mid
    wide_reg = jnp.dot(
        spread(fields * octet, fields, True, octet), outw_ref[...], preferred_element_type=F32
    )
    row_reg = lax.broadcasted_iota(jnp.int32, wide_reg.shape, 0) % octet
    for r in range(octet):
        fout[:, r * channels : (r + 1) * channels] = jnp.where(row_reg == r, wide_reg, 0.0).astype(
            BF
        )
    for k in range(2):
        copies[2 + k].wait()
        for m in range(MEMB):
            lat[k, :, m * cells : (m + 1) * cells] = (
                noise[k, m].astype(F32).reshape(flat, cells) * SIGMAS[0]
            )

    halo_copy.wait_recv()
    inside = jnp.where(top_half, tile > 0, tile < tiles - 1)
    from_neighbour = jnp.where(inside, halo_in[0:cin, :].astype(F32), 0.0)
    row_below = cv[:, half_rows, :].astype(F32)
    row_above = cv[:, half_rows - 1, :].astype(F32)
    edges = jnp.concatenate(
        [
            jnp.where(top_half, from_neighbour, row_above),
            jnp.where(top_half, row_below, from_neighbour),
        ],
        axis=1,
    ).astype(BF)
    lifted_edges = silu_of_half(jnp.dot(lift_bf, edges, preferred_element_type=F32))
    lifted[:channels, :cells] = lifted_edges[:, :cells]
    lifted[:channels, cells:] = lifted[octet * channels : (octet + 1) * channels, :cells]
    lifted[(octet + 1) * channels :, :cells] = lifted[channels : 2 * channels, cells:]
    lifted[(octet + 1) * channels :, cells:] = lifted_edges[:, cells:]
    column = lax.broadcasted_iota(jnp.int32, (channels, cells), 1)
    for r in range(octet):
        taps = jnp.dot(
            wconv[...],
            lifted[r * channels : (r + 3) * channels, :],
            preferred_element_type=F32,
        )
        for side in range(2):
            span = slice(side * cells, (side + 1) * cells)
            left = pltpu.roll(taps[:channels, span], 1, 1)
            right = pltpu.roll(taps[2 * channels :, span], cells - 1, 1)
            total = (
                taps[channels : 2 * channels, span]
                + jnp.where(column == 0, 0.0, left)
                + jnp.where(column == cells - 1, 0.0, right)
            )
            feat[r * channels : (r + 1) * channels, span] = silu_of_half(total)
    produced = jnp.dot(fout[...], feat[...], preferred_element_type=F32)
    condition = jnp.concatenate(
        [
            produced[c * octet : (c + 1) * octet, side * cells : (side + 1) * cells]
            for c in range(fields)
            for side in range(2)
        ],
        axis=0,
    ).astype(BF)

    lane_row = lax.broadcasted_iota(jnp.int32, (half_rows, cells), 1)
    listed = jnp.full((half_rows, cells), -1.0, F32)
    count = jnp.int32(MEMB)
    for j in range(REACH):
        listed = jnp.where(lane_row == j, dest_ref[0, j].astype(F32), listed)
        count = count + jnp.where(dest_ref[0, j] >= 0, 1, 0)
    cond[0, :flat, :] = condition
    cond[0, flat:, :] = listed.astype(BF)
    cond_copies = []
    for o in range(1, REACH):
        copy = pltpu.make_async_remote_copy(
            src_ref=cond.at[0],
            dst_ref=cond.at[o],
            send_sem=send_sem.at[o],
            recv_sem=recv_sem.at[o],
            device_id={"tile": ahead[o]},
            device_id_type=MESH,
        )
        copy.start()
        cond_copies.append(copy)

    def denoise_step(group, position):
        latent = lat[group]
        stacked = jnp.concatenate([(latent * pick(position, 0)).astype(BF), gx[group]], axis=0)
        piece_rows = 4 * channels
        for r in range(half_rows // 4):
            block = slice(r * piece_rows, (r + 1) * piece_rows)
            hid1[block, :] = silu_of_half(
                jnp.dot(ein[block, :], stacked, preferred_element_type=F32)
            )
        for r in range(half_rows // 2):
            block = slice(2 * r * channels, 2 * (r + 1) * channels)
            hid2[block, :] = silu_of_half(
                jnp.dot(emid[...], hid1[block, :], preferred_element_type=F32)
            )
        found = jnp.dot(eout[...], hid2[...], preferred_element_type=F32)
        lat[group] = latent * pick(position, 1) + found * pick(position, 2)

    def run_steps(group, low, high):
        def step(position, carry):
            denoise_step(group, position)
            return carry

        lax.fori_loop(low, high, step, 0)

    gx[0] = jnp.concatenate([condition] * MEMB, axis=1)
    run_steps(0, 0, NSTEP // 2)

    for copy in cond_copies:
        copy.wait_recv()
    me = tile.astype(F32)
    named = [
        jnp.max(jnp.where(cond[o, flat:, :].astype(F32) == me, 1.0, 0.0)) for o in range(REACH)
    ]
    chosen = []
    for o in range(REACH):
        rank = jnp.float32(0.0)
        for other in range(REACH):
            if other != o:
                rank = rank + jnp.where(behind[other] < behind[o], named[other], 0.0)
        chosen.append([jnp.where(rank == k, named[o], 0.0) for k in range(SLOTS)])
    for k in range(SLOTS):
        served = cond[0, :flat, :].astype(F32) * chosen[0][k]
        for o in range(1, REACH):
            served = served + cond[o, :flat, :].astype(F32) * chosen[o][k]
        gx[1, :, k * cells : (k + 1) * cells] = served.astype(BF)
    run_steps(1, 0, NSTEP)

    extra = lat[1] + gx[1].astype(F32)
    for o in range(REACH):
        sample = extra[:, :cells] * chosen[o][0]
        for k in range(1, SLOTS):
            sample = sample + extra[:, k * cells : (k + 1) * cells] * chosen[o][k]
        piece[o] = sample
    piece_copies = []
    for o in range(1, REACH):
        copy = pltpu.make_async_remote_copy(
            src_ref=piece.at[o],
            dst_ref=arrived.at[o],
            send_sem=send_sem.at[REACH + o],
            recv_sem=recv_sem.at[REACH + o],
            device_id={"tile": behind[o]},
            device_id_type=MESH,
        )
        copy.start()
        piece_copies.append(copy)

    run_steps(0, NSTEP // 2, NSTEP)

    base = lat[0] + gx[0].astype(F32)
    total = piece[0]
    square = total * total
    for m in range(MEMB):
        sample = base[:, m * cells : (m + 1) * cells]
        total = total + sample
        square = square + sample * sample
    for o, copy in enumerate(piece_copies, 1):
        copy.wait_recv()
        sample = arrived[o]
        total = total + sample
        square = square + sample * sample
    members = count.astype(F32)
    mean = total / members
    variance = square / members - mean * mean

    swap_out[...] = jnp.where(top_half, variance, mean)
    swap = pltpu.make_async_remote_copy(
        src_ref=swap_out,
        dst_ref=swap_in,
        send_sem=send_sem.at[REACH],
        recv_sem=recv_sem.at[REACH],
        device_id={"section": 1 - section},
        device_id_type=MESH,
    )
    swap.start()
    kept = jnp.where(top_half, mean, variance)
    out_ref[0, :, pl.ds(first, half_rows), :] = kept.reshape(fields, half_rows, cells)
    halo_copy.wait_send()
    for copy in cond_copies + piece_copies:
        copy.wait_send()
    swap.wait()
    second = pl.multiple_of((1 - section) * half_rows, half_rows)
    out_ref[0, :, pl.ds(second, half_rows), :] = swap_in[...].reshape(fields, half_rows, cells)


def body(tiles, *arrays):
    (coarse, lift, conv, outw, din, dmid, dout, base, slot, dest) = arrays
    cin, rows, cells = coarse.shape
    channels = lift.shape[0]
    fields = outw.shape[0]
    half = rows // 2
    flat = fields * half
    vmem = pl.BlockSpec(memory_space=pltpu.VMEM)
    anywhere = pl.BlockSpec(memory_space=pl.ANY)
    scratch = [
        pltpu.VMEM(coarse.shape, BF),
        pltpu.VMEM(conv.shape, BF),
        pltpu.VMEM((2, MEMB, fields, half, cells), BF),
        pltpu.VMEM((16, cells), BF),
        pltpu.VMEM((16, cells), BF),
        pltpu.VMEM(((half // 2 + 2) * channels, 2 * cells), BF),
        pltpu.VMEM((3 * channels, 3 * channels), BF),
        pltpu.VMEM((half // 2 * channels, 2 * cells), BF),
        pltpu.VMEM((fields * half // 2, half // 2 * channels), BF),
        pltpu.VMEM((half * channels, 2 * flat), BF),
        pltpu.VMEM((2 * channels, 2 * channels), BF),
        pltpu.VMEM((flat, half * channels), BF),
        pltpu.VMEM((half * channels, MEMB * cells), BF),
        pltpu.VMEM((half * channels, MEMB * cells), BF),
        pltpu.VMEM((2, flat, MEMB * cells), F32),
        pltpu.VMEM((REACH, flat + 16, cells), BF),
        pltpu.VMEM((2, flat, MEMB * cells), BF),
        pltpu.VMEM((REACH, flat, cells), F32),
        pltpu.VMEM((REACH, flat, cells), F32),
        pltpu.VMEM((flat, cells), F32),
        pltpu.VMEM((flat, cells), F32),
        pltpu.SemaphoreType.DMA((4,)),
        pltpu.SemaphoreType.DMA((2 * REACH,)),
        pltpu.SemaphoreType.DMA((2 * REACH,)),
    ]
    return pl.pallas_call(
        functools.partial(kernel, tiles),
        out_shape=jax.ShapeDtypeStruct((1, fields, rows, cells), F32),
        in_specs=[anywhere, vmem, anywhere, vmem, vmem, vmem, vmem, anywhere, anywhere]
        + [pl.BlockSpec(memory_space=pltpu.SMEM)],
        out_specs=vmem,
        scratch_shapes=scratch,
        compiler_params=pltpu.CompilerParams(
            collective_id=0, has_side_effects=True, vmem_limit_bytes=48 * 2**20
        ),
        name="ensemble",
    )(*arrays)


def solution(mesh):
    in_specs = (
        P(None, "tile", None),
        P(),
        P(),
        P(),
        P(),
        P(),
        P(),
        P(None, None, "tile", None),
        P(None, None, "tile", None),
        P("tile", None),
    )
    out_specs = P("section", None, "tile", None)
    return jax.shard_map(
        functools.partial(body, mesh.shape["tile"]),
        mesh=mesh,
        in_specs=in_specs,
        out_specs=out_specs,
        check_vma=False,
    )
```

profile of v0, /device:TPU:1, one launch (start us, length us, event | category | flops | bytes accessed | tf_op | source)
XLA Modules:
  0.0 51.1 jit_solution(11086864671196923906)
XLA Ops:
  0.0 0.0 copy-start.4
  0.0 0.0 copy-start.8
  0.0 0.8 %copy.11.lift_ref = bf16[128,12]{1,0:T(8,128)(2,1)S(1)} copy(bf16[128,12]{0,1:T(8,128)(2,1)} %param.11) | data formatting | bytes 6144 | tf_op args[1]
  0.8 0.0 copy-done.8
  0.8 0.0 copy-start.5
  0.9 0.0 copy-start.6
  0.9 0.0 copy-start.7
  0.9 0.1 copy.12.din_ref
  1.0 0.0 copy-done.4
  1.0 0.5 %copy-done.5 = bf16[4,128]{1,0:T(4,128)(2,1)S(1)} copy-done((bf16[4,128]{1,0:T(4,128)(2,1)S(1)}, bf16[4,128]{1,0:T(4,128)(2,1)}, u32[]{:S(2)}) %copy-start.5) | copy-done | bytes 1048
  1.5 0.0 copy-done.6
  1.5 0.0 copy-done.7
  1.5 0.0 copy-start
  1.5 1.0 %copy-done = bf16[3,3,128,128]{3,2,1,0:T(8,128)(2,1)S(1)} copy-done((bf16[3,3,128,128]{3,2,1,0:T(8,128)(2,1)S(1)}, bf16[3,3,128,128]{3,2,1,0:T(8,128)(2,1)}, u32[]{:S(2)}) %copy-start) | copy-done | bytes 294936
  2.5 0.0 copy-start.1
  2.5 0.9 %copy-done.1 = bf16[4,4,32,128]{3,2,1,0:T(8,128)(2,1)S(1)} copy-done((bf16[4,4,32,128]{3,2,1,0:T(8,128)(2,1)S(1)}, bf16[4,4,32,128]{3,2,1,0:T(8,128)(2,1)}, u32[]{:S(2)}) %copy-start.1) | copy-done | bytes 131096
  3.4 0.0 copy-start.2
  3.4 0.9 %copy-done.2 = bf16[4,4,32,128]{3,2,1,0:T(8,128)(2,1)S(1)} copy-done((bf16[4,4,32,128]{3,2,1,0:T(8,128)(2,1)S(1)}, bf16[4,4,32,128]{3,2,1,0:T(8,128)(2,1)}, u32[]{:S(2)}) %copy-start.2) | copy-done | bytes 131096
  4.3 0.0 copy-start.3
  4.3 0.9 %copy-done.3 = bf16[12,32,128]{2,1,0:T(8,128)(2,1)S(1)} copy-done((bf16[12,32,128]{2,1,0:T(8,128)(2,1)S(1)}, bf16[12,32,128]{2,1,0:T(8,128)(2,1)}, u32[]{:S(2)}) %copy-start.3) | copy-done | bytes 98328
  5.2 45.2 %ensemble.1 = f32[1,4,32,128]{3,2,1,0:T(8,128)S(1)} custom-call(bf16[12,32,128]{2,1,0:T(8,128)(2,1)S(1)} %copy-done.3, bf16[128,12]{1,0:T(8,128)(2,1)S(1)} %copy.11.lift_ref, bf16[3,3,128,128]{3,2,1,0:T(8,128)(2,1)S(1)} %copy-done, bf16[4,128]{1,0:T(4,128)(2,1)S(1)} %copy-done.5, bf16[128,8]{1,0:T(8,128)(2,1)S(1)} %copy.12.din_ref, ...), custom_call_target="tpu_custom_call" | custom-call | tf_op jit(solution)/shard_map/ensemble/pallas_call | solution.py:421
  50.4 0.6 %copy.14 = f32[1,4,32,128]{3,2,1,0:T(8,128)} copy(f32[1,4,32,128]{3,2,1,0:T(8,128)S(1)} %ensemble.1) | data formatting | bytes 131072
Async XLA Ops:
  0.0 1.0 %copy-start.4 = (bf16[128,128]{1,0:T(8,128)(2,1)S(1)}, bf16[128,128]{1,0:T(8,128)(2,1)}, u32[]{:S(2)}) copy-start(bf16[128,128]{1,0:T(8,128)(2,1)} %dmid_ref.1) | copy-start | bytes 98308
  0.0 0.8 %copy-start.8 = (bf16[128,8]{0,1:T(8,128)(2,1)S(1)}, bf16[128,8]{0,1:T(8,128)(2,1)}, u32[]{:S(2)}) copy-start(bf16[128,8]{0,1:T(8,128)(2,1)} %param.14) | copy-start | bytes 6148
  0.8 0.7 %copy-start.5 = (bf16[4,128]{1,0:T(4,128)(2,1)S(1)}, bf16[4,128]{1,0:T(4,128)(2,1)}, u32[]{:S(2)}) copy-start(bf16[4,128]{1,0:T(4,128)(2,1)} %outw_ref.1) | copy-start | bytes 3076
  0.9 0.7 %copy-start.6 = (bf16[4,128]{1,0:T(4,128)(2,1)S(1)}, bf16[4,128]{1,0:T(4,128)(2,1)}, u32[]{:S(2)}) copy-start(bf16[4,128]{1,0:T(4,128)(2,1)} %dout_ref.1) | copy-start | bytes 3076
  0.9 0.7 %copy-start.7 = (s32[1,8]{1,0:T(1,128)S(1)}, s32[1,8]{1,0:T(1,128)}, u32[]{:S(2)}) copy-start(s32[1,8]{1,0:T(1,128)} %dest_ref.1) | copy-start | bytes 100
  1.5 1.0 %copy-start = (bf16[3,3,128,128]{3,2,1,0:T(8,128)(2,1)S(1)}, bf16[3,3,128,128]{3,2,1,0:T(8,128)(2,1)}, u32[]{:S(2)}) copy-start(bf16[3,3,128,128]{3,2,1,0:T(8,128)(2,1)} %conv_ref.1) | copy-start | bytes 884740
  2.5 0.9 %copy-start.1 = (bf16[4,4,32,128]{3,2,1,0:T(8,128)(2,1)S(1)}, bf16[4,4,32,128]{3,2,1,0:T(8,128)(2,1)}, u32[]{:S(2)}) copy-start(bf16[4,4,32,128]{3,2,1,0:T(8,128)(2,1)} %base_ref.1) | copy-start | bytes 393220
  3.4 0.9 %copy-start.2 = (bf16[4,4,32,128]{3,2,1,0:T(8,128)(2,1)S(1)}, bf16[4,4,32,128]{3,2,1,0:T(8,128)(2,1)}, u32[]{:S(2)}) copy-start(bf16[4,4,32,128]{3,2,1,0:T(8,128)(2,1)} %slot_ref.1) | copy-start | bytes 393220
  4.3 0.9 %copy-start.3 = (bf16[12,32,128]{2,1,0:T(8,128)(2,1)S(1)}, bf16[12,32,128]{2,1,0:T(8,128)(2,1)}, u32[]{:S(2)}) copy-start(bf16[12,32,128]{2,1,0:T(8,128)(2,1)} %coarse_ref.1) | copy-start | bytes 294916
where the time goes:
time: 51.3 us; the launch traced here: 51.1 us
  Pallas kernels  45.2 us (88%)
  local copies, waits for them, and re-layouts  5.81 us (11%)
    pallas_call x1, Pallas kernels, body(): pl.pallas_call(functools.partial(kernel, tiles), out_shape=jax.ShapeDtype...  45.2 us
    unnamed x21, local copies, waits for them, and re-layouts  5.81 us

commit v1 on v0

--- a/solution.py
+++ b/solution.py
@@ -80,6 +80,12 @@
     out_ref,
     cv,
     wraw,
+    lift_v,
+    outw_v,
+    din_v,
+    dmid_v,
+    dout_v,
+    dest_s,
     noise,
     halo_out,
     halo_in,
@@ -107,10 +113,10 @@
     tile = lax.axis_index("tile")
     half_rows = out_ref.shape[2] // 2
     cells = out_ref.shape[3]
-    channels = din_ref.shape[0]
+    channels = din_ref.shape[1]
     fields = out_ref.shape[1]
     flat = fields * half_rows
-    cin = lift_ref.shape[1]
+    cin = lift_ref.shape[0]
     octet = half_rows // 2
     first = pl.multiple_of(section * half_rows, half_rows)
 
@@ -123,6 +129,12 @@
         pltpu.make_async_copy(
             slot_ref.at[:, :, pl.ds(first, half_rows), :], noise.at[1], local_sem.at[3]
         ),
+        pltpu.make_async_copy(lift_ref, lift_v, local_sem.at[4]),
+        pltpu.make_async_copy(outw_ref, outw_v, local_sem.at[5]),
+        pltpu.make_async_copy(din_ref, din_v, local_sem.at[6]),
+        pltpu.make_async_copy(dmid_ref, dmid_v, local_sem.at[7]),
+        pltpu.make_async_copy(dout_ref, dout_v, local_sem.at[8]),
+        pltpu.make_async_copy(dest_ref, dest_s, local_sem.at[9]),
     ]
     for copy in copies:
         copy.start()
@@ -157,8 +169,10 @@
     )
     halo_copy.start()
 
-    lift_half = lift_ref[...].astype(F32) * 0.5
-    lift_bf = lift_half.astype(BF)
+    for copy in copies[4:]:
+        copy.wait()
+    lift_half = lift_v[...].astype(F32) * 0.5
+    lift_bf = lift_half.T.astype(BF)
     wide = jnp.dot(lift_bf, spread(cin, cin * octet, False, octet), preferred_element_type=F32)
     lane = lax.broadcasted_iota(jnp.int32, wide.shape, 1) % octet
     own = cv[:, pl.ds(first, half_rows), :].astype(F32)
@@ -182,25 +196,25 @@
             )
     wide_in = (
         jnp.dot(
-            din_ref[...], spread(2 * fields, 2 * flat, False, half_rows), preferred_element_type=F32
+            din_v[...].astype(F32).T.astype(BF), spread(2 * fields, 2 * flat, False, half_rows), preferred_element_type=F32
         )
         * 0.5
     )
     lane_in = lax.broadcasted_iota(jnp.int32, wide_in.shape, 1) % half_rows
     wide_out = jnp.dot(
-        spread(flat, fields, True, half_rows), dout_ref[...], preferred_element_type=F32
+        spread(flat, fields, True, half_rows), dout_v[...], preferred_element_type=F32
     )
     row_out = lax.broadcasted_iota(jnp.int32, wide_out.shape, 0) % half_rows
     for r in range(half_rows):
         block = slice(r * channels, (r + 1) * channels)
         ein[block, :] = jnp.where(lane_in == r, wide_in, 0.0).astype(BF)
         eout[:, block] = jnp.where(row_out == r, wide_out, 0.0).astype(BF)
-    mid = (dmid_ref[...].astype(F32) * 0.5).astype(BF)
+    mid = (dmid_v[...].astype(F32) * 0.5).astype(BF)
     emid[...] = jnp.zeros(emid.shape, BF)
     emid[:channels, :channels] = mid
     emid[channels:, channels:] = mid
     wide_reg = jnp.dot(
-        spread(fields * octet, fields, True, octet), outw_ref[...], preferred_element_type=F32
+        spread(fields * octet, fields, True, octet), outw_v[...], preferred_element_type=F32
     )
     row_reg = lax.broadcasted_iota(jnp.int32, wide_reg.shape, 0) % octet
     for r in range(octet):
@@ -262,8 +276,8 @@
     listed = jnp.full((half_rows, cells), -1.0, F32)
     count = jnp.int32(MEMB)
     for j in range(REACH):
-        listed = jnp.where(lane_row == j, dest_ref[0, j].astype(F32), listed)
-        count = count + jnp.where(dest_ref[0, j] >= 0, 1, 0)
+        listed = jnp.where(lane_row == j, dest_s[0, j].astype(F32), listed)
+        count = count + jnp.where(dest_s[0, j] >= 0, 1, 0)
     cond[0, :flat, :] = condition
     cond[0, flat:, :] = listed.astype(BF)
     cond_copies = []
@@ -387,14 +401,22 @@
     (coarse, lift, conv, outw, din, dmid, dout, base, slot, dest) = arrays
     cin, rows, cells = coarse.shape
     channels = lift.shape[0]
+    lift = lift.T
+    din = din.T
     fields = outw.shape[0]
     half = rows // 2
     flat = fields * half
     vmem = pl.BlockSpec(memory_space=pltpu.VMEM)
-    anywhere = pl.BlockSpec(memory_space=pl.ANY)
+    in_hbm = pl.BlockSpec(memory_space=pltpu.HBM)
     scratch = [
         pltpu.VMEM(coarse.shape, BF),
         pltpu.VMEM(conv.shape, BF),
+        pltpu.VMEM(lift.shape, BF),
+        pltpu.VMEM(outw.shape, BF),
+        pltpu.VMEM(din.shape, BF),
+        pltpu.VMEM(dmid.shape, BF),
+        pltpu.VMEM(dout.shape, BF),
+        pltpu.SMEM(dest.shape, jnp.int32),
         pltpu.VMEM((2, MEMB, fields, half, cells), BF),
         pltpu.VMEM((16, cells), BF),
         pltpu.VMEM((16, cells), BF),
@@ -414,22 +436,21 @@
         pltpu.VMEM((REACH, flat, cells), F32),
         pltpu.VMEM((flat, cells), F32),
         pltpu.VMEM((flat, cells), F32),
-        pltpu.SemaphoreType.DMA((4,)),
+        pltpu.SemaphoreType.DMA((10,)),
         pltpu.SemaphoreType.DMA((2 * REACH,)),
         pltpu.SemaphoreType.DMA((2 * REACH,)),
     ]
     return pl.pallas_call(
         functools.partial(kernel, tiles),
         out_shape=jax.ShapeDtypeStruct((1, fields, rows, cells), F32),
-        in_specs=[anywhere, vmem, anywhere, vmem, vmem, vmem, vmem, anywhere, anywhere]
-        + [pl.BlockSpec(memory_space=pltpu.SMEM)],
+        in_specs=[in_hbm] * 10,
         out_specs=vmem,
         scratch_shapes=scratch,
         compiler_params=pltpu.CompilerParams(
-            collective_id=0, has_side_effects=True, vmem_limit_bytes=48 * 2**20
+            collective_id=0, has_side_effects=True, vmem_limit_bytes=60 * 2**20
         ),
         name="ensemble",
-    )(*arrays)
+    )(coarse, lift, conv, outw, din, dmid, dout, base, slot, dest)
 
 
 def solution(mesh):

time: 51.3 us -> 46.8 us (0.912)
  local copies, waits for them, and re-layouts: 5.81 us -> 1.47 us
    unnamed x21 -> x1, local copies, waits for them, and re-layouts: 5.81 us -> 1.47 us
where the time goes in v1:
time: 46.8 us; the launch traced here: 46.7 us
  Pallas kernels  45.2 us (97%)
  local copies, waits for them, and re-layouts  1.47 us (3%)
    pallas_call x1, Pallas kernels, body(): pl.pallas_call(functools.partial(kernel, tiles), out_shape=jax.ShapeDtype...  45.2 us
    unnamed x1, local copies, waits for them, and re-layouts  1.47 us

profile of v1, /device:TPU:1, one launch (start us, length us, event | category | flops | bytes accessed | tf_op | source)
XLA Modules:
  0.0 46.7 jit_solution(2756086453195536928)
XLA Ops:
  0.0 45.2 %ensemble.1 = f32[1,4,32,128]{3,2,1,0:T(8,128)} custom-call(bf16[12,32,128]{2,1,0:T(8,128)(2,1)} %coarse_ref.1, bf16[12,128]{1,0:T(8,128)(2,1)} %bitcast.2, bf16[3,3,128,128]{3,2,1,0:T(8,128)(2,1)} %conv_ref.1, bf16[4,128]{1,0:T(4,128)(2,1)} %outw_ref.1, bf16[8,128]{1,0:T(8,128)(2,1)} %bitcast.3, bf16[128,128]{1,0:T(8,128)(2,1)} %dmid_ref.1, ...), custom_call_target="tpu_custom_call" | custom-call | tf_op jit(solution)/shard_map/ensemble/pallas_call | solution.py:443
  45.2 1.5 %copy.12 = f32[1,4,32,128]{3,2,1,0:T(8,128)} copy(f32[1,4,32,128]{3,2,1,0:T(8,128)} %ensemble.1) | data formatting | bytes 131072

commit v2 on v1

--- a/solution.py
+++ b/solution.py
@@ -100,6 +100,7 @@
     hid2,
     lat,
     cond,
+    listing,
     gx,
     piece,
     arrived,
@@ -143,7 +144,7 @@
     behind = [lax.rem(tile + tiles - o, tiles) for o in range(REACH)]
 
     barrier = pltpu.get_barrier_semaphore()
-    for o in range(1, REACH):
+    for o in range(REACH - 1, 0, -1):
         for other in (ahead[o], behind[o]):
             pl.semaphore_signal(barrier, inc=1, device_id={"tile": other}, device_id_type=MESH)
     pl.semaphore_signal(
@@ -156,18 +157,6 @@
     first_row = cv[:, 0, :].astype(F32)
     halo_out[...] = jnp.zeros(halo_out.shape, BF)
     halo_out[0:cin, :] = jnp.where(top_half, last_row, first_row).astype(BF)
-
-    pl.semaphore_wait(barrier, 2 * (REACH - 1) + 1)
-    halo_target = lax.rem(jnp.where(top_half, tile + 1, tile + tiles - 1), tiles)
-    halo_copy = pltpu.make_async_remote_copy(
-        src_ref=halo_out,
-        dst_ref=halo_in,
-        send_sem=send_sem.at[0],
-        recv_sem=recv_sem.at[0],
-        device_id={"tile": halo_target},
-        device_id_type=MESH,
-    )
-    halo_copy.start()
 
     for copy in copies[4:]:
         copy.wait()
@@ -194,25 +183,6 @@
             wconv[b * channels : (b + 1) * channels, a * channels : (a + 1) * channels] = (
                 (wraw[a, b].astype(F32) * 0.5).T.astype(BF)
             )
-    wide_in = (
-        jnp.dot(
-            din_v[...].astype(F32).T.astype(BF), spread(2 * fields, 2 * flat, False, half_rows), preferred_element_type=F32
-        )
-        * 0.5
-    )
-    lane_in = lax.broadcasted_iota(jnp.int32, wide_in.shape, 1) % half_rows
-    wide_out = jnp.dot(
-        spread(flat, fields, True, half_rows), dout_v[...], preferred_element_type=F32
-    )
-    row_out = lax.broadcasted_iota(jnp.int32, wide_out.shape, 0) % half_rows
-    for r in range(half_rows):
-        block = slice(r * channels, (r + 1) * channels)
-        ein[block, :] = jnp.where(lane_in == r, wide_in, 0.0).astype(BF)
-        eout[:, block] = jnp.where(row_out == r, wide_out, 0.0).astype(BF)
-    mid = (dmid_v[...].astype(F32) * 0.5).astype(BF)
-    emid[...] = jnp.zeros(emid.shape, BF)
-    emid[:channels, :channels] = mid
-    emid[channels:, channels:] = mid
     wide_reg = jnp.dot(
         spread(fields * octet, fields, True, octet), outw_v[...], preferred_element_type=F32
     )
@@ -221,12 +191,59 @@
         fout[:, r * channels : (r + 1) * channels] = jnp.where(row_reg == r, wide_reg, 0.0).astype(
             BF
         )
-    for k in range(2):
-        copies[2 + k].wait()
-        for m in range(MEMB):
-            lat[k, :, m * cells : (m + 1) * cells] = (
-                noise[k, m].astype(F32).reshape(flat, cells) * SIGMAS[0]
+    pl.semaphore_wait(barrier, 2 * (REACH - 1) + 1)
+    halo_target = lax.rem(jnp.where(top_half, tile + 1, tile + tiles - 1), tiles)
+    halo_copy = pltpu.make_async_remote_copy(
+        src_ref=halo_out,
+        dst_ref=halo_in,
+        send_sem=send_sem.at[0],
+        recv_sem=recv_sem.at[0],
+        device_id={"tile": halo_target},
+        device_id_type=MESH,
+    )
+    halo_copy.start()
+
+    lane_row = lax.broadcasted_iota(jnp.int32, (8, cells), 1)
+    listed = jnp.full((8, cells), -1.0, F32)
+    count = jnp.int32(MEMB)
+    for j in range(REACH):
+        listed = jnp.where(lane_row == j, dest_s[0, j].astype(F32), listed)
+        count = count + jnp.where(dest_s[0, j] >= 0, 1, 0)
+    listing[0] = listed
+    list_copies = []
+    for o in range(REACH - 1, 0, -1):
+        copy = pltpu.make_async_remote_copy(
+            src_ref=listing.at[0],
+            dst_ref=listing.at[o],
+            send_sem=send_sem.at[2 * REACH + o],
+            recv_sem=recv_sem.at[2 * REACH + o],
+            device_id={"tile": ahead[o]},
+            device_id_type=MESH,
+        )
+        copy.start()
+        list_copies.append(copy)
+
+    column = lax.broadcasted_iota(jnp.int32, (channels, cells), 1)
+
+    def convolve(r):
+        taps = jnp.dot(
+            wconv[...],
+            lifted[r * channels : (r + 3) * channels, :],
+            preferred_element_type=F32,
+        )
+        for side in range(2):
+            span = slice(side * cells, (side + 1) * cells)
+            left = pltpu.roll(taps[:channels, span], 1, 1)
+            right = pltpu.roll(taps[2 * channels :, span], cells - 1, 1)
+            total = (
+                taps[channels : 2 * channels, span]
+                + jnp.where(column == 0, 0.0, left)
+                + jnp.where(column == cells - 1, 0.0, right)
             )
+            feat[r * channels : (r + 1) * channels, span] = silu_of_half(total)
+
+    for r in range(1, octet - 1):
+        convolve(r)
 
     halo_copy.wait_recv()
     inside = jnp.where(top_half, tile > 0, tile < tiles - 1)
@@ -245,23 +262,8 @@
     lifted[:channels, cells:] = lifted[octet * channels : (octet + 1) * channels, :cells]
     lifted[(octet + 1) * channels :, :cells] = lifted[channels : 2 * channels, cells:]
     lifted[(octet + 1) * channels :, cells:] = lifted_edges[:, cells:]
-    column = lax.broadcasted_iota(jnp.int32, (channels, cells), 1)
-    for r in range(octet):
-        taps = jnp.dot(
-            wconv[...],
-            lifted[r * channels : (r + 3) * channels, :],
-            preferred_element_type=F32,
-        )
-        for side in range(2):
-            span = slice(side * cells, (side + 1) * cells)
-            left = pltpu.roll(taps[:channels, span], 1, 1)
-            right = pltpu.roll(taps[2 * channels :, span], cells - 1, 1)
-            total = (
-                taps[channels : 2 * channels, span]
-                + jnp.where(column == 0, 0.0, left)
-                + jnp.where(column == cells - 1, 0.0, right)
-            )
-            feat[r * channels : (r + 1) * channels, span] = silu_of_half(total)
+    convolve(0)
+    convolve(octet - 1)
     produced = jnp.dot(fout[...], feat[...], preferred_element_type=F32)
     condition = jnp.concatenate(
         [
@@ -272,16 +274,9 @@
         axis=0,
     ).astype(BF)
 
-    lane_row = lax.broadcasted_iota(jnp.int32, (half_rows, cells), 1)
-    listed = jnp.full((half_rows, cells), -1.0, F32)
-    count = jnp.int32(MEMB)
-    for j in range(REACH):
-        listed = jnp.where(lane_row == j, dest_s[0, j].astype(F32), listed)
-        count = count + jnp.where(dest_s[0, j] >= 0, 1, 0)
-    cond[0, :flat, :] = condition
-    cond[0, flat:, :] = listed.astype(BF)
+    cond[0] = condition
     cond_copies = []
-    for o in range(1, REACH):
+    for o in range(REACH - 1, 0, -1):
         copy = pltpu.make_async_remote_copy(
             src_ref=cond.at[0],
             dst_ref=cond.at[o],
@@ -292,6 +287,34 @@
         )
         copy.start()
         cond_copies.append(copy)
+
+    wide_in = (
+        jnp.dot(
+            din_v[...].astype(F32).T.astype(BF),
+            spread(2 * fields, 2 * flat, False, half_rows),
+            preferred_element_type=F32,
+        )
+        * 0.5
+    )
+    lane_in = lax.broadcasted_iota(jnp.int32, wide_in.shape, 1) % half_rows
+    wide_out = jnp.dot(
+        spread(flat, fields, True, half_rows), dout_v[...], preferred_element_type=F32
+    )
+    row_out = lax.broadcasted_iota(jnp.int32, wide_out.shape, 0) % half_rows
+    for r in range(half_rows):
+        block = slice(r * channels, (r + 1) * channels)
+        ein[block, :] = jnp.where(lane_in == r, wide_in, 0.0).astype(BF)
+        eout[:, block] = jnp.where(row_out == r, wide_out, 0.0).astype(BF)
+    mid = (dmid_v[...].astype(F32) * 0.5).astype(BF)
+    emid[...] = jnp.zeros(emid.shape, BF)
+    emid[:channels, :channels] = mid
+    emid[channels:, channels:] = mid
+    for k in range(2):
+        copies[2 + k].wait()
+        for m in range(MEMB):
+            lat[k, :, m * cells : (m + 1) * cells] = (
+                noise[k, m].astype(F32).reshape(flat, cells) * SIGMAS[0]
+            )
 
     def denoise_step(group, position):
         latent = lat[group]
@@ -318,13 +341,13 @@
         lax.fori_loop(low, high, step, 0)
 
     gx[0] = jnp.concatenate([condition] * MEMB, axis=1)
-    run_steps(0, 0, NSTEP // 2)
-
-    for copy in cond_copies:
+    run_steps(0, 0, 4)
+
+    for copy in list_copies + cond_copies:
         copy.wait_recv()
     me = tile.astype(F32)
     named = [
-        jnp.max(jnp.where(cond[o, flat:, :].astype(F32) == me, 1.0, 0.0)) for o in range(REACH)
+        jnp.max(jnp.where(listing[o] == me, 1.0, 0.0)) for o in range(REACH)
     ]
     chosen = []
     for o in range(REACH):
@@ -334,20 +357,23 @@
                 rank = rank + jnp.where(behind[other] < behind[o], named[other], 0.0)
         chosen.append([jnp.where(rank == k, named[o], 0.0) for k in range(SLOTS)])
     for k in range(SLOTS):
-        served = cond[0, :flat, :].astype(F32) * chosen[0][k]
+        served = cond[0].astype(F32) * chosen[0][k]
         for o in range(1, REACH):
-            served = served + cond[o, :flat, :].astype(F32) * chosen[o][k]
+            served = served + cond[o].astype(F32) * chosen[o][k]
         gx[1, :, k * cells : (k + 1) * cells] = served.astype(BF)
     run_steps(1, 0, NSTEP)
 
     extra = lat[1] + gx[1].astype(F32)
-    for o in range(REACH):
+    own_sample = None
+    piece_copies = []
+    for o in range(REACH - 1, -1, -1):
         sample = extra[:, :cells] * chosen[o][0]
         for k in range(1, SLOTS):
             sample = sample + extra[:, k * cells : (k + 1) * cells] * chosen[o][k]
-        piece[o] = sample
-    piece_copies = []
-    for o in range(1, REACH):
+        if o == 0:
+            own_sample = sample
+            continue
+        piece[o] = sample.astype(BF)
         copy = pltpu.make_async_remote_copy(
             src_ref=piece.at[o],
             dst_ref=arrived.at[o],
@@ -359,18 +385,18 @@
         copy.start()
         piece_copies.append(copy)
 
-    run_steps(0, NSTEP // 2, NSTEP)
+    run_steps(0, 4, NSTEP)
 
     base = lat[0] + gx[0].astype(F32)
-    total = piece[0]
+    total = own_sample
     square = total * total
     for m in range(MEMB):
         sample = base[:, m * cells : (m + 1) * cells]
         total = total + sample
         square = square + sample * sample
-    for o, copy in enumerate(piece_copies, 1):
-        copy.wait_recv()
-        sample = arrived[o]
+    for o in range(1, REACH):
+        piece_copies[REACH - 1 - o].wait_recv()
+        sample = arrived[o].astype(F32)
         total = total + sample
         square = square + sample * sample
     members = count.astype(F32)
@@ -390,7 +416,7 @@
     kept = jnp.where(top_half, mean, variance)
     out_ref[0, :, pl.ds(first, half_rows), :] = kept.reshape(fields, half_rows, cells)
     halo_copy.wait_send()
-    for copy in cond_copies + piece_copies:
+    for copy in list_copies + cond_copies + piece_copies:
         copy.wait_send()
     swap.wait()
     second = pl.multiple_of((1 - section) * half_rows, half_rows)
@@ -430,15 +456,16 @@
         pltpu.VMEM((half * channels, MEMB * cells), BF),
         pltpu.VMEM((half * channels, MEMB * cells), BF),
         pltpu.VMEM((2, flat, MEMB * cells), F32),
-        pltpu.VMEM((REACH, flat + 16, cells), BF),
+        pltpu.VMEM((REACH, flat, cells), BF),
+        pltpu.VMEM((REACH, 8, cells), F32),
         pltpu.VMEM((2, flat, MEMB * cells), BF),
-        pltpu.VMEM((REACH, flat, cells), F32),
-        pltpu.VMEM((REACH, flat, cells), F32),
+        pltpu.VMEM((REACH, flat, cells), BF),
+        pltpu.VMEM((REACH, flat, cells), BF),
         pltpu.VMEM((flat, cells), F32),
         pltpu.VMEM((flat, cells), F32),
         pltpu.SemaphoreType.DMA((10,)),
-        pltpu.SemaphoreType.DMA((2 * REACH,)),
-        pltpu.SemaphoreType.DMA((2 * REACH,)),
+        pltpu.SemaphoreType.DMA((3 * REACH,)),
+        pltpu.SemaphoreType.DMA((3 * REACH,)),
     ]
     return pl.pallas_call(
         functools.partial(kernel, tiles),
@@ -447,10 +474,15 @@
         out_specs=vmem,
         scratch_shapes=scratch,
         compiler_params=pltpu.CompilerParams(
-            collective_id=0, has_side_effects=True, vmem_limit_bytes=60 * 2**20
+            collective_id=0, has_side_effects=True, vmem_limit_bytes=48 * 2**20
         ),
         name="ensemble",
-    )(coarse, lift, conv, outw, din, dmid, dout, base, slot, dest)
+    )(
+        *[
+            pltpu.with_memory_space_constraint(array, pltpu.HBM)
+            for array in (coarse, lift, conv, outw, din, dmid, dout, base, slot, dest)
+        ]
+    )
 
 
 def solution(mesh):

time: 46.8 us -> 40.8 us (0.87)
  Pallas kernels: 45.2 us -> 40.1 us
  local copies, waits for them, and re-layouts: 1.47 us -> 0.63 us
    pallas_call x1, Pallas kernels: 45.2 us -> 40.1 us  [body(): pl.pallas_call(functools.partial(kernel, tiles), out_shape=jax.ShapeDtype...]
    unnamed x1, local copies, waits for them, and re-layouts: 1.47 us -> 0.63 us
where the time goes in v2:
time: 40.8 us
  Pallas kernels  40.1 us (98%)
  local copies, waits for them, and re-layouts  0.63 us (2%)
    pallas_call x1, Pallas kernels, body(): pl.pallas_call(functools.partial(kernel, tiles), out_shape=jax.ShapeDtype...  40.1 us

profile of v2, /device:TPU:1, one launch (start us, length us, event | category | flops | bytes accessed | tf_op | source)
XLA Modules:
  0.0 40.8 jit_solution(4623302317398030341)
XLA Ops:
  0.0 40.1 %ensemble.1 = f32[1,4,32,128]{3,2,1,0:T(8,128)S(1)} custom-call(bf16[12,32,128]{2,1,0:T(8,128)(2,1)} %coarse_ref.1, bf16[12,128]{1,0:T(8,128)(2,1)} %bitcast.2, bf16[3,3,128,128]{3,2,1,0:T(8,128)(2,1)} %conv_ref.1, bf16[4,128]{1,0:T(4,128)(2,1)} %outw_ref.1, bf16[8,128]{1,0:T(8,128)(2,1)} %bitcast.3, bf16[128,128]{1,0:T(8,128)(2,1)} %dmid_ref.1, ...), custom_call_target="tpu_custom_call" | custom-call | tf_op jit(solution)/shard_map/ensemble/pallas_call | solution.py:470
  40.1 0.6 %copy.12 = f32[1,4,32,128]{3,2,1,0:T(8,128)} copy(f32[1,4,32,128]{3,2,1,0:T(8,128)S(1)} %ensemble.1) | data formatting | bytes 131072

commit v3 on v2

--- a/solution.py
+++ b/solution.py
@@ -100,6 +100,7 @@
     hid2,
     lat,
     cond,
+    edge,
     listing,
     gx,
     piece,
@@ -210,50 +211,30 @@
         listed = jnp.where(lane_row == j, dest_s[0, j].astype(F32), listed)
         count = count + jnp.where(dest_s[0, j] >= 0, 1, 0)
     listing[0] = listed
-    list_copies = []
-    for o in range(REACH - 1, 0, -1):
-        copy = pltpu.make_async_remote_copy(
-            src_ref=listing.at[0],
-            dst_ref=listing.at[o],
-            send_sem=send_sem.at[2 * REACH + o],
-            recv_sem=recv_sem.at[2 * REACH + o],
-            device_id={"tile": ahead[o]},
-            device_id_type=MESH,
-        )
-        copy.start()
-        list_copies.append(copy)
-
-    column = lax.broadcasted_iota(jnp.int32, (channels, cells), 1)
-
-    def convolve(r):
-        taps = jnp.dot(
-            wconv[...],
-            lifted[r * channels : (r + 3) * channels, :],
-            preferred_element_type=F32,
-        )
-        for side in range(2):
-            span = slice(side * cells, (side + 1) * cells)
-            left = pltpu.roll(taps[:channels, span], 1, 1)
-            right = pltpu.roll(taps[2 * channels :, span], cells - 1, 1)
-            total = (
-                taps[channels : 2 * channels, span]
-                + jnp.where(column == 0, 0.0, left)
-                + jnp.where(column == cells - 1, 0.0, right)
+
+    def send_ahead(buffer, bank):
+        started = []
+        for o in range(REACH - 1, 0, -1):
+            copy = pltpu.make_async_remote_copy(
+                src_ref=buffer.at[0],
+                dst_ref=buffer.at[o],
+                send_sem=send_sem.at[bank * REACH + o],
+                recv_sem=recv_sem.at[bank * REACH + o],
+                device_id={"tile": ahead[o]},
+                device_id_type=MESH,
             )
-            feat[r * channels : (r + 1) * channels, span] = silu_of_half(total)
-
-    for r in range(1, octet - 1):
-        convolve(r)
-
-    halo_copy.wait_recv()
-    inside = jnp.where(top_half, tile > 0, tile < tiles - 1)
-    from_neighbour = jnp.where(inside, halo_in[0:cin, :].astype(F32), 0.0)
+            copy.start()
+            started.append(copy)
+        return started
+
+    list_copies = send_ahead(listing, 2)
+
     row_below = cv[:, half_rows, :].astype(F32)
     row_above = cv[:, half_rows - 1, :].astype(F32)
     edges = jnp.concatenate(
         [
-            jnp.where(top_half, from_neighbour, row_above),
-            jnp.where(top_half, row_below, from_neighbour),
+            jnp.where(top_half, 0.0, row_above),
+            jnp.where(top_half, row_below, 0.0),
         ],
         axis=1,
     ).astype(BF)
@@ -262,10 +243,28 @@
     lifted[:channels, cells:] = lifted[octet * channels : (octet + 1) * channels, :cells]
     lifted[(octet + 1) * channels :, :cells] = lifted[channels : 2 * channels, cells:]
     lifted[(octet + 1) * channels :, cells:] = lifted_edges[:, cells:]
-    convolve(0)
-    convolve(octet - 1)
+    column = lax.broadcasted_iota(jnp.int32, (channels, cells), 1)
+
+    def combine(taps):
+        left = pltpu.roll(taps[:channels], 1, 1)
+        right = pltpu.roll(taps[2 * channels :], cells - 1, 1)
+        return silu_of_half(
+            taps[channels : 2 * channels]
+            + jnp.where(column == 0, 0.0, left)
+            + jnp.where(column == cells - 1, 0.0, right)
+        )
+
+    for r in range(octet):
+        taps = jnp.dot(
+            wconv[...],
+            lifted[r * channels : (r + 3) * channels, :],
+            preferred_element_type=F32,
+        )
+        for side in range(2):
+            span = slice(side * cells, (side + 1) * cells)
+            feat[r * channels : (r + 1) * channels, span] = combine(taps[:, span])
     produced = jnp.dot(fout[...], feat[...], preferred_element_type=F32)
-    condition = jnp.concatenate(
+    cond[0] = jnp.concatenate(
         [
             produced[c * octet : (c + 1) * octet, side * cells : (side + 1) * cells]
             for c in range(fields)
@@ -274,19 +273,42 @@
         axis=0,
     ).astype(BF)
 
-    cond[0] = condition
-    cond_copies = []
-    for o in range(REACH - 1, 0, -1):
-        copy = pltpu.make_async_remote_copy(
-            src_ref=cond.at[0],
-            dst_ref=cond.at[o],
-            send_sem=send_sem.at[o],
-            recv_sem=recv_sem.at[o],
-            device_id={"tile": ahead[o]},
-            device_id_type=MESH,
-        )
-        copy.start()
-        cond_copies.append(copy)
+    cond_copies = send_ahead(cond, 1)
+    halo_copy.wait_recv()
+    inside = jnp.where(top_half, tile > 0, tile < tiles - 1)
+    from_neighbour = jnp.where(inside, halo_in[0:cin, :].astype(F32), 0.0).astype(BF)
+    halo = silu_of_half(jnp.dot(lift_bf, from_neighbour, preferred_element_type=F32))
+
+    def rows_at(low, high):
+        upper = lifted[low * channels : (low + 1) * channels, :cells]
+        lower = lifted[high * channels : (high + 1) * channels, cells:]
+        return jnp.where(top_half, upper, lower)
+
+    around = jnp.concatenate(
+        [
+            jnp.where(top_half, halo, lifted[(octet - 1) * channels : octet * channels, cells:]),
+            rows_at(1, octet),
+            jnp.where(top_half, lifted[2 * channels : 3 * channels, :cells], halo),
+        ],
+        axis=0,
+    )
+    beside = combine(jnp.dot(wconv[...], around, preferred_element_type=F32))
+    edge[0, :fields, :] = (
+        jnp.dot(outw_v[...], beside, preferred_element_type=F32).astype(BF).astype(F32)
+    )
+    edge[0, fields:, :] = jnp.zeros((edge.shape[1] - fields, cells), F32)
+    edge_copies = send_ahead(edge, 3)
+
+    row_of = lax.broadcasted_iota(jnp.int32, (flat, cells), 0) % half_rows
+    edge_row = jnp.where(top_half, 0, half_rows - 1)
+
+    def with_edge(most, row):
+        repeated = jnp.concatenate(
+            [jnp.broadcast_to(row[c : c + 1, :], (half_rows, cells)) for c in range(fields)], axis=0
+        )
+        return jnp.where(row_of == edge_row, repeated, most)
+
+    condition = with_edge(cond[0].astype(F32), edge[0]).astype(BF)
 
     wide_in = (
         jnp.dot(
@@ -341,9 +363,9 @@
         lax.fori_loop(low, high, step, 0)
 
     gx[0] = jnp.concatenate([condition] * MEMB, axis=1)
-    run_steps(0, 0, 4)
-
-    for copy in list_copies + cond_copies:
+    run_steps(0, 0, 5)
+
+    for copy in list_copies:
         copy.wait_recv()
     me = tile.astype(F32)
     named = [
@@ -356,11 +378,15 @@
             if other != o:
                 rank = rank + jnp.where(behind[other] < behind[o], named[other], 0.0)
         chosen.append([jnp.where(rank == k, named[o], 0.0) for k in range(SLOTS)])
+    for copy in cond_copies + edge_copies:
+        copy.wait_recv()
     for k in range(SLOTS):
         served = cond[0].astype(F32) * chosen[0][k]
+        served_row = edge[0] * chosen[0][k]
         for o in range(1, REACH):
             served = served + cond[o].astype(F32) * chosen[o][k]
-        gx[1, :, k * cells : (k + 1) * cells] = served.astype(BF)
+            served_row = served_row + edge[o] * chosen[o][k]
+        gx[1, :, k * cells : (k + 1) * cells] = with_edge(served, served_row).astype(BF)
     run_steps(1, 0, NSTEP)
 
     extra = lat[1] + gx[1].astype(F32)
@@ -377,15 +403,15 @@
         copy = pltpu.make_async_remote_copy(
             src_ref=piece.at[o],
             dst_ref=arrived.at[o],
-            send_sem=send_sem.at[REACH + o],
-            recv_sem=recv_sem.at[REACH + o],
+            send_sem=send_sem.at[4 * REACH + o],
+            recv_sem=recv_sem.at[4 * REACH + o],
             device_id={"tile": behind[o]},
             device_id_type=MESH,
         )
         copy.start()
         piece_copies.append(copy)
 
-    run_steps(0, 4, NSTEP)
+    run_steps(0, 5, NSTEP)
 
     base = lat[0] + gx[0].astype(F32)
     total = own_sample
@@ -416,7 +442,7 @@
     kept = jnp.where(top_half, mean, variance)
     out_ref[0, :, pl.ds(first, half_rows), :] = kept.reshape(fields, half_rows, cells)
     halo_copy.wait_send()
-    for copy in list_copies + cond_copies + piece_copies:
+    for copy in list_copies + cond_copies + edge_copies + piece_copies:
         copy.wait_send()
     swap.wait()
     second = pl.multiple_of((1 - section) * half_rows, half_rows)
@@ -458,14 +484,15 @@
         pltpu.VMEM((2, flat, MEMB * cells), F32),
         pltpu.VMEM((REACH, flat, cells), BF),
         pltpu.VMEM((REACH, 8, cells), F32),
+        pltpu.VMEM((REACH, 8, cells), F32),
         pltpu.VMEM((2, flat, MEMB * cells), BF),
         pltpu.VMEM((REACH, flat, cells), BF),
         pltpu.VMEM((REACH, flat, cells), BF),
         pltpu.VMEM((flat, cells), F32),
         pltpu.VMEM((flat, cells), F32),
         pltpu.SemaphoreType.DMA((10,)),
-        pltpu.SemaphoreType.DMA((3 * REACH,)),
-        pltpu.SemaphoreType.DMA((3 * REACH,)),
+        pltpu.SemaphoreType.DMA((5 * REACH,)),
+        pltpu.SemaphoreType.DMA((5 * REACH,)),
     ]
     return pl.pallas_call(
         functools.partial(kernel, tiles),

time: 40.8 us -> 40.1 us (0.983)
  Pallas kernels: 40.1 us -> 39.4 us
    pallas_call x1, Pallas kernels: 40.1 us -> 39.4 us  [body(): pl.pallas_call(functools.partial(kernel, tiles), out_shape=jax.ShapeDtype...]
where the time goes in v3:
time: 40.1 us; the launch traced here: 40 us
  Pallas kernels  39.4 us (98%)
  local copies, waits for them, and re-layouts  0.63 us (2%)
    pallas_call x1, Pallas kernels, body(): pl.pallas_call(functools.partial(kernel, tiles), out_shape=jax.ShapeDtype...  39.4 us

profile of v3, /device:TPU:1, one launch (start us, length us, event | category | flops | bytes accessed | tf_op | source)
XLA Modules:
  0.0 40.0 jit_solution(13129678897418006199)
XLA Ops:
  0.0 39.4 %ensemble.1 = f32[1,4,32,128]{3,2,1,0:T(8,128)S(1)} custom-call(bf16[12,32,128]{2,1,0:T(8,128)(2,1)} %coarse_ref.1, bf16[12,128]{1,0:T(8,128)(2,1)} %bitcast.2, bf16[3,3,128,128]{3,2,1,0:T(8,128)(2,1)} %conv_ref.1, bf16[4,128]{1,0:T(4,128)(2,1)} %outw_ref.1, bf16[8,128]{1,0:T(8,128)(2,1)} %bitcast.3, bf16[128,128]{1,0:T(8,128)(2,1)} %dmid_ref.1, ...), custom_call_target="tpu_custom_call" | custom-call | tf_op jit(solution)/shard_map/ensemble/pallas_call | solution.py:497
  39.4 0.6 %copy.12 = f32[1,4,32,128]{3,2,1,0:T(8,128)} copy(f32[1,4,32,128]{3,2,1,0:T(8,128)S(1)} %ensemble.1) | data formatting | bytes 131072

commit v4 on v3

--- a/solution.py
+++ b/solution.py
@@ -320,13 +320,14 @@
     )
     lane_in = lax.broadcasted_iota(jnp.int32, wide_in.shape, 1) % half_rows
     wide_out = jnp.dot(
-        spread(flat, fields, True, half_rows), dout_v[...], preferred_element_type=F32
-    )
-    row_out = lax.broadcasted_iota(jnp.int32, wide_out.shape, 0) % half_rows
+        spread(fields * octet, fields, True, octet), dout_v[...], preferred_element_type=F32
+    )
+    row_out = lax.broadcasted_iota(jnp.int32, wide_out.shape, 0) % octet
     for r in range(half_rows):
         block = slice(r * channels, (r + 1) * channels)
         ein[block, :] = jnp.where(lane_in == r, wide_in, 0.0).astype(BF)
-        eout[:, block] = jnp.where(row_out == r, wide_out, 0.0).astype(BF)
+        if r < octet:
+            eout[:, block] = jnp.where(row_out == r, wide_out, 0.0).astype(BF)
     mid = (dmid_v[...].astype(F32) * 0.5).astype(BF)
     emid[...] = jnp.zeros(emid.shape, BF)
     emid[:channels, :channels] = mid
@@ -352,7 +353,23 @@
             hid2[block, :] = silu_of_half(
                 jnp.dot(emid[...], hid1[block, :], preferred_element_type=F32)
             )
-        found = jnp.dot(eout[...], hid2[...], preferred_element_type=F32)
+        span = octet * channels
+        parts = [
+            jnp.dot(
+                eout[:, :span],
+                hid2[side * span : (side + 1) * span, :],
+                preferred_element_type=F32,
+            )
+            for side in range(2)
+        ]
+        found = jnp.concatenate(
+            [
+                parts[side][c * octet : (c + 1) * octet]
+                for c in range(fields)
+                for side in range(2)
+            ],
+            axis=0,
+        )
         lat[group] = latent * pick(position, 1) + found * pick(position, 2)
 
     def run_steps(group, low, high):
@@ -478,7 +495,7 @@
         pltpu.VMEM((fields * half // 2, half // 2 * channels), BF),
         pltpu.VMEM((half * channels, 2 * flat), BF),
         pltpu.VMEM((2 * channels, 2 * channels), BF),
-        pltpu.VMEM((flat, half * channels), BF),
+        pltpu.VMEM((flat // 2, half // 2 * channels), BF),
         pltpu.VMEM((half * channels, MEMB * cells), BF),
         pltpu.VMEM((half * channels, MEMB * cells), BF),
         pltpu.VMEM((2, flat, MEMB * cells), F32),

time: 40.1 us -> 40 us (level)
  no operation moved by 1% of the time
where the time goes in v4:
time: 40 us; the launch traced here: 39.9 us
  Pallas kernels  39.2 us (98%)
  local copies, waits for them, and re-layouts  0.63 us (2%)
    pallas_call x1, Pallas kernels, body(): pl.pallas_call(functools.partial(kernel, tiles), out_shape=jax.ShapeDtype...  39.2 us

profile of v4, /device:TPU:1, one launch (start us, length us, event | category | flops | bytes accessed | tf_op | source)
XLA Modules:
  0.0 39.9 jit_solution(13362340890659979957)
XLA Ops:
  0.0 39.2 %ensemble.1 = f32[1,4,32,128]{3,2,1,0:T(8,128)S(1)} custom-call(bf16[12,32,128]{2,1,0:T(8,128)(2,1)} %coarse_ref.1, bf16[12,128]{1,0:T(8,128)(2,1)} %bitcast.2, bf16[3,3,128,128]{3,2,1,0:T(8,128)(2,1)} %conv_ref.1, bf16[4,128]{1,0:T(4,128)(2,1)} %outw_ref.1, bf16[8,128]{1,0:T(8,128)(2,1)} %bitcast.3, bf16[128,128]{1,0:T(8,128)(2,1)} %dmid_ref.1, ...), custom_call_target="tpu_custom_call" | custom-call | tf_op jit(solution)/shard_map/ensemble/pallas_call | solution.py:514
  39.2 0.6 %copy.12 = f32[1,4,32,128]{3,2,1,0:T(8,128)} copy(f32[1,4,32,128]{3,2,1,0:T(8,128)S(1)} %ensemble.1) | data formatting | bytes 131072
